TPU v7x, 256 devices: a whole 4x4x8 slice. The times are simulated.
256 devices in a mesh: loop: 16 (over y, x), dp: 16 (over z, core).
Axes of the slice: x: 4, y: 4, z: 8, core: 2. Of those that a mesh axis runs over, the one named last changes fastest.
Arguments:
- tokens: bfloat16 [3584, 8192], P('dp', 'loop'), may hold values from -8 to 8
- weight: bfloat16 [8192, 14336], P('loop', 'dp'), as said below
- rounding: float32 [8192, 14336], P('loop', 'dp'), may hold values from -6 to 6
- floor_codes: int32 [8192, 14336], P('loop', 'dp'), may hold values from -1 to 15
- scale_codes: int32 [14336], P('dp'), may hold values from 12 to 15
- zero_codes: int32 [14336], P('dp'), may hold values from 0 to 15
- block_mask: int32 [128, 224], P('loop', 'dp'), may hold values from 0 to 1, as said below
Outputs:
- refined: float32 [8192, 14336], P('loop', 'dp')
Inputs may be any that keep to these rules, and one draw needn't show every extreme that they name: weight equals scales times (floor_codes - zero_point + a fraction in [0, 1)), then is rounded to bfloat16. `block_mask`: the share of surviving blocks differs between column blocks.
All inputs are finite; a program needn't handle non-finite values.
Results may differ from a plain program's by a relative error of at most 0.019.
Values may be sent and summed in bfloat16 or wider, within the bound.
A program may use at most 128 MiB of HBM per device.

v0:
```python
import jax
import jax.numpy as jnp
from jax import lax
from jax.sharding import PartitionSpec as P

BLOCK = 64
ITERS = 2


step_rate = 20.0
reg_weight = 0.05
base_scale = 0.02


def expand(block_mask):
    row_blocks, col_blocks = block_mask.shape
    spread = jnp.broadcast_to(block_mask[:, None, :, None], (row_blocks, BLOCK, col_blocks, BLOCK))
    return spread.reshape(row_blocks * BLOCK, col_blocks * BLOCK).astype(jnp.float32)


def token_product(token_rows, scaled_err):
    return lax.dot_general(
        token_rows, scaled_err, (((0,), (0,)), ((), ())), preferred_element_type=jnp.float32
    )


def per_device(tokens, weight, rounding, floor_codes, scale_codes, zero_codes, block_mask):
    gathered = lax.all_gather(tokens, "dp", axis=0, tiled=True)
    token_count = gathered.shape[0]
    scales = base_scale * jnp.exp2(scale_codes.astype(jnp.float32) * 0.25)
    zero_point = zero_codes.astype(jnp.float32)
    kept_mask = expand(block_mask)
    floors = floor_codes.astype(jnp.float32)
    in_range = ((floor_codes >= 0) & (floor_codes <= 14)).astype(jnp.float32)
    target = weight.astype(jnp.float32)
    for iteration in range(ITERS):
        relaxed = jax.nn.sigmoid(rounding)
        levels = jnp.clip(floors + relaxed, 0.0, 15.0)
        w_delta = (kept_mask * (scales[None, :] * (levels - zero_point[None, :]) - target)).astype(
            jnp.bfloat16
        )
        partial_sum = jnp.dot(gathered, w_delta, preferred_element_type=jnp.float32)
        residual = lax.psum(partial_sum.astype(jnp.bfloat16), "loop").astype(jnp.float32)
        scaled_err = (2.0 / token_count * residual).astype(jnp.bfloat16)
        gradient = token_product(gathered, scaled_err)
        centered = 2.0 * relaxed - 1.0
        descent = gradient * scales[None, :] * in_range - reg_weight * 8.0 * centered**3
        rounding = rounding - step_rate * kept_mask * descent * relaxed * (1.0 - relaxed)
    return rounding


def solution(mesh):
    placed = (
        P("dp", "loop"),
        P("loop", "dp"),
        P("loop", "dp"),
        P("loop", "dp"),
        P("dp"),
        P("dp"),
        P("loop", "dp"),
    )
    return jax.shard_map(
        per_device, mesh=mesh, in_specs=placed, out_specs=P("loop", "dp"), check_vma=False
    )
```

profile of v0, /device:TPU:2, one launch (start us, length us, event | category | flops | bytes accessed | tf_op | source)
XLA Modules:
  0.0 363.7 jit_solution(10741293267602168995)
XLA Ops:
  6.5 0.0 all-gather.2.cloned.1.call-start
  6.5 0.7 all-gather.2.cloned.1.call-update
  7.3 0.0 all-reduce.3.cloned.1.call-start
  7.3 0.7 convert_element_type.50
  8.0 0.1 copy.8
  8.1 2.1 broadcast_in_dim.2
  10.2 4.4 %convert_element_type.51 = f32[512,896]{0,1:T(8,128)} reshape(f32[8,64,14,64]{1,0,3,2:T(8,128)} %broadcast_in_dim.2) | data formatting | bytes 3670016 | tf_op jit(solution)/shard_map/convert_element_type | solution.py:18
  14.6 1.8 copy.9
  16.4 0.0 copy-start.1
  16.4 0.0 copy-start.3
  16.4 2.8 copy.14
  19.2 0.0 copy-done.1
  19.2 0.0 copy-start.4
  19.2 1.3 copy.13
  20.5 0.0 copy-done.3
  20.5 0.0 copy-done.4
  20.5 32.9 %all-gather.2.cloned.1.call-done = bf16[3584,512]{1,0:T(8,128)(2,1)} async-done(((bf16[224,512]{1,0:T(8,128)(2,1)}), bf16[3584,512]{1,0:T(8,128)(2,1)}) %all-gather.2.cloned.1.call-update) | async-done | bytes 3670032 | tf_op jit(solution)/shard_map/all_gather | solution.py:28
  53.4 10.1 %fusion.4 = bf16[3584,896]{0,1:T(8,128)(2,1)} fusion(bf16[3584,512]{1,0:T(8,128)(2,1)} %all-gather.2.cloned.1.call-done, f32[512,896]{0,1:T(8,128)} %convert_element_type.51, bf16[512,896]{0,1:T(8,128)(2,1)} %copy.13, s32[512,896]{0,1:T(8,128)S(1)} %copy.9, f32[512,896]{0,1:T(8,128)} %copy.14, f32[896]{0:T(1024)S(1)} %convert_element_type.54, ...), kind=kOutput, calls=%fused_computation.8 | convolution fusion | flops 3297050624 | bytes 16522240 | tf_op jit(solution)/shard_map/dot_general | solution.py:42
  63.5 0.0 all-reduce.3.cloned.1.call-update
  63.5 0.2 all-reduce.5.cloned.1.call-start
  63.8 0.4 compare_and_fusion
  64.1 0.0 copy-start.2
  64.1 131.6 %all-reduce.3.cloned.1.call-done = bf16[3584,896]{0,1:T(8,128)(2,1)} async-done(((bf16[3584,896]{0,1:T(8,128)(2,1)}), bf16[3584,896]{0,1:T(8,128)(2,1)}) %all-reduce.3.cloned.1.call-update) | async-done | bytes 6422544 | tf_op jit(solution)/shard_map/psum | solution.py:43
  195.8 0.0 copy-start
  195.8 0.0 copy-start.5
  195.8 9.5 %fusion.15 = f32[512,896]{0,1:T(8,128)S(1)} fusion(f32[512,896]{0,1:T(8,128)} %copy.14, pred[512,896]{0,1:T(32,128)(4,1)S(1)} %compare_and_fusion, f32[512,896]{0,1:T(8,128)} %convert_element_type.51, bf16[3584,512]{1,0:T(8,128)(2,1)} %all-gather.2.cloned.1.call-done, bf16[3584,896]{0,1:T(8,128)(2,1)} %all-reduce.3.cloned.1.call-done, ...), kind=kOutput, calls=%fused_computation.23 | convolution fusion | flops 3305766912 | bytes 16059904 | tf_op jit(solution)/shard_map/dot_general | solution.py:22
  205.3 0.0 copy-start.6
  205.3 1.2 copy-done.6
  206.5 0.0 copy-done.2
  206.5 0.0 copy-done
  206.5 0.0 copy-done.5
  206.5 6.2 %fusion.5 = bf16[3584,896]{0,1:T(8,128)(2,1)} fusion(bf16[3584,512]{1,0:T(8,128)(2,1)S(1)} %copy-done.5, f32[512,896]{0,1:T(8,128)S(1)} %copy-done, bf16[512,896]{0,1:T(8,128)(2,1)S(1)} %copy-done.2, s32[512,896]{0,1:T(8,128)S(1)} %copy.9, f32[512,896]{0,1:T(8,128)S(1)} %fusion.15, f32[896]{0:T(1024)S(1)} %convert_element_type.54, ...), kind=kOutput, calls=%fused_computation.9 | convolution fusion | flops 3297050624 | bytes 16522240 | tf_op jit(solution)/shard_map/dot_general | solution.py:42
  212.7 0.0 all-reduce.5.cloned.1.call-update
  212.7 133.4 %all-reduce.5.cloned.1.call-done = bf16[3584,896]{0,1:T(8,128)(2,1)} async-done(((bf16[3584,896]{0,1:T(8,128)(2,1)}), bf16[3584,896]{0,1:T(8,128)(2,1)}) %all-reduce.5.cloned.1.call-update) | async-done | bytes 6422544 | tf_op jit(solution)/shard_map/psum | solution.py:43
  346.1 9.4 %fusion.21 = f32[512,896]{0,1:T(8,128)S(1)} fusion(f32[512,896]{0,1:T(8,128)} %copy-done.6, pred[512,896]{0,1:T(32,128)(4,1)S(1)} %compare_and_fusion, f32[512,896]{0,1:T(8,128)} %convert_element_type.51, bf16[3584,512]{1,0:T(8,128)(2,1)} %all-gather.2.cloned.1.call-done, bf16[3584,896]{0,1:T(8,128)(2,1)} %all-reduce.5.cloned.1.call-done, ...), kind=kOutput, calls=%fused_computation.29 | convolution fusion | flops 3305766912 | bytes 16059904 | tf_op jit(solution)/shard_map/dot_general | solution.py:22
  355.5 1.7 copy.15
  (2 shorter events, 0.0 us)
Async XLA Ops:
  6.5 46.9 %all-gather.2.cloned.1.call-start = ((), (), s32[]{:S(2)}) async-start(), calls=%async_computation | async-start | bytes 3899392 | tf_op jit(solution)/shard_map/all_gather | solution.py:28
  7.3 188.5 %all-reduce.3.cloned.1.call-start = ((), (), s32[]{:S(2)}) async-start(), calls=%async_computation.1 | async-start | bytes 12845056 | tf_op jit(solution)/shard_map/psum | solution.py:43
  16.4 2.8 copy-start.1
  16.4 4.1 %copy-start.3 = (s32[896]{0:T(1024)S(1)}, s32[896]{0:T(1024)}, u32[]{:S(2)}) copy-start(s32[896]{0:T(1024)} %param.12) | copy-start | bytes 10756
  19.2 1.3 copy-start.4
  63.5 282.5 %all-reduce.5.cloned.1.call-start = ((), (), s32[]{:S(2)}) async-start(), calls=%async_computation.2 | async-start | bytes 12845056 | tf_op jit(solution)/shard_map/psum | solution.py:43
  64.1 142.4 %copy-start.2 = (bf16[512,896]{0,1:T(8,128)(2,1)S(1)}, bf16[512,896]{0,1:T(8,128)(2,1)}, u32[]{:S(2)}) copy-start(bf16[512,896]{0,1:T(8,128)(2,1)} %copy.13) | copy-start | bytes 2752516
  195.8 10.8 %copy-start = (f32[512,896]{0,1:T(8,128)S(1)}, f32[512,896]{0,1:T(8,128)}, u32[]{:S(2)}) copy-start(f32[512,896]{0,1:T(8,128)} %convert_element_type.51) | copy-start | bytes 5505028
  195.8 10.8 %copy-start.5 = (bf16[3584,512]{1,0:T(8,128)(2,1)S(1)}, bf16[3584,512]{1,0:T(8,128)(2,1)}, u32[]{:S(2)}) copy-start(bf16[3584,512]{1,0:T(8,128)(2,1)} %all-gather.2.cloned.1.call-done) | copy-start | bytes 11010052
  205.3 1.2 copy-start.6
Sparse Core Ops, SparseCore 0:
  9.2 44.2 all-gather.1
  63.7 132.0 all-reduce.2
  212.8 133.2 all-reduce.4
where the time goes:
time: 365 us; the launch traced here: 364 us
  waiting for transfers between devices  299 us (82%)
  matrix products  35.1 us (10%)
  local copies, waits for them, and re-layouts  15.4 us (4%)
  between operations  13.2 us (4%)
    psum x2, waiting for transfers between devices, per_device(): lax.psum(partial_sum.astype(jnp.bfloat16), 'loop').astype(jnp.float32)  265 us
    all_gather x1, waiting for transfers between devices, per_device(): gathered = lax.all_gather(tokens, 'dp', axis=0, tiled=True)  32.9 us
    dot_general x2, matrix products, token_product(): lax.dot_general(token_rows, scaled_err, (((0,), (0,)), ((), ())), preferr...  18.9 us
    dot_general x2, matrix products, per_device(): partial_sum = jnp.dot(gathered, w_delta, preferred_element_type=jnp.float32)  16.2 us
  transfers between devices with their start and end apart: 3, of which 3 were waited for; matrix products, arithmetic and copies ran while one was open for 4% of the time, Pallas kernels for 0%

commit v1 on v0

v1 whole, which is shorter than its diff:
```python
import jax
import jax.numpy as jnp
from jax import lax
from jax.experimental import pallas as pl
from jax.experimental.pallas import tpu as pltpu
from jax.sharding import PartitionSpec as P

MESH = pl.DeviceIdType.MESH
BLOCK = 64
ITERS = 2
RING = 4
DEPTH = 8

step_rate = 20.0
reg_weight = 0.05
base_scale = 0.02

ROWS = 512
COLS = 896
TOKENS = 3584
PIECE = 112
WAVE = 4 * PIECE
SPLIT = 64
HALF = ROWS // 2
TILE = 16


def kernel(
    tok, wt, v_in, fl, sc, zp, km, out,
    X, W, RS, RCA, RCB, RFP, RFM, E, Racc, Gacc, GS, GCA, GCB, GFP, GFM,
    x1_send, x1_recv, z_send, z_recv, w_send, w_recv, r_send, r_recv, e_send, e_recv, g_send, g_recv,
):
    loop = lax.axis_index("loop")
    dp = lax.axis_index("dp")
    y, x = loop // 4, lax.rem(loop, 4)
    z, c = dp // 2, lax.rem(dp, 2)
    g = x * (1 - c) + y * c
    r = y * (1 - c) + x * c

    def device(gp, rp):
        return (gp * (1 + 3 * c) + rp * (4 - 3 * c), dp)

    g_next = device(lax.rem(g + 1, 4), r)
    g_prev = device(lax.rem(g + 3, 4), r)
    r_next = device(g, lax.rem(r + 1, 4))
    r_prev = device(g, lax.rem(r + 3, 4))
    z_next = (loop, lax.rem(z + 1, DEPTH) * 2 + c)
    z_prev = (loop, lax.rem(z + DEPTH - 1, DEPTH) * 2 + c)

    pending = []

    def send(src, dst, send_sem, recv_sem, to):
        copy = pltpu.make_async_remote_copy(
            src_ref=src, dst_ref=dst, send_sem=send_sem, recv_sem=recv_sem, device_id=to, device_id_type=MESH
        )
        copy.start()
        pending.append(copy)
        return copy

    def arrived(ref, sem):
        pltpu.make_async_copy(ref, ref, sem).wait()

    exchange = []
    for j in range(2):
        goal = 2 * c + j
        for role in range(2):
            if role == 0:
                to = (y * 4 + goal, z * 2)
                slot = lax.rem(x - goal + 4, 4)
                mine = (goal - x) * (goal - x) + c
            else:
                to = (goal * 4 + x, z * 2 + 1)
                slot = lax.rem(y - goal + 4, 4)
                mine = (goal - y) * (goal - y) + (1 - c)
            src = tok.at[pl.ds(j * PIECE, PIECE), :]
            dst = X.at[slot, pl.ds(0, PIECE), :]
            sem = x1_recv.at[slot]
            remote = pltpu.make_async_remote_copy(
                src_ref=src, dst_ref=dst, send_sem=x1_send.at[2 * j + role], recv_sem=sem,
                device_id=to, device_id_type=MESH,
            )
            local = pltpu.make_async_copy(src, dst, sem)
            exchange.append((mine, remote))

            @pl.when(mine == 0)
            def _():
                local.start()

            @pl.when(mine != 0)
            def _():
                remote.start()

    def piece(slot, half):
        return X.at[pl.ds(2 * half, 2), pl.ds(slot * PIECE, PIECE), :]

    def z_forward(sign, slot, half):
        to = z_next if sign > 0 else z_prev
        if sign > 0:
            there = {0: 1, 1: 3, 3: 5, 5: 7}[slot]
        else:
            there = {0: 2, 2: 4, 4: 6, 6: 7}[slot]
        index = 2 * there + half
        return send(piece(slot, half), piece(there, half), z_send.at[index], z_recv.at[index], to)

    def z_wait(slot, half):
        arrived(piece(slot, half), z_recv.at[2 * slot + half])

    scale = sc[...]
    zero = zp[...]

    def delta(tile, v):
        rows = pl.ds(pl.multiple_of(tile * TILE, TILE), TILE)
        kept = km[pl.ds(tile // (BLOCK // TILE), 1), :]
        relaxed = jax.nn.sigmoid(v)
        levels = jnp.clip(fl[rows, :].astype(jnp.float32) + relaxed, 0.0, 15.0)
        return (kept * (scale * (levels - zero) - wt[rows, :].astype(jnp.float32))).astype(jnp.bfloat16)

    def first_delta():
        def body(tile, carry):
            rows = pl.ds(pl.multiple_of(tile * TILE, TILE), TILE)
            W[0, 0, rows, :] = delta(tile, v_in[rows, :])
            return carry

        lax.fori_loop(0, ROWS // TILE, body, 0)

    def update(it):
        old = v_in if it == 0 else out

        def body(tile, carry):
            rows = pl.ds(pl.multiple_of(tile * TILE, TILE), TILE)
            v = old[rows, :]
            gradient = (
                Gacc[0, rows, :] + GFP[it, rows, :].astype(jnp.float32) + GFM[it, rows, :].astype(jnp.float32)
            )
            relaxed = jax.nn.sigmoid(v)
            codes = fl[rows, :]
            in_range = ((codes >= 0) & (codes <= 14)).astype(jnp.float32)
            kept = km[pl.ds(tile // (BLOCK // TILE), 1), :]
            centered = 2.0 * relaxed - 1.0
            descent = gradient * scale * in_range - reg_weight * 8.0 * (centered * centered * centered)
            v = v - step_rate * kept * descent * relaxed * (1.0 - relaxed)
            out[rows, :] = v
            if it + 1 < ITERS:
                W[it + 1, 0, rows, :] = delta(tile, v)
            return carry

        lax.fori_loop(0, ROWS // TILE, body, 0)

    TOP, LOW = pl.ds(0, HALF), pl.ds(HALF, HALF)

    def w_copy(it, here, there, rows, index, to):
        return send(W.at[it, here, rows, :], W.at[it, there, rows, :], w_send.at[it, index], w_recv.at[it, index], to)

    def w_start(it):
        w_copy(it, 0, 3, TOP, 0, g_next)
        w_copy(it, 0, 1, LOW, 1, g_prev)
        w_copy(it, 0, 3, LOW, 2, g_next)
        w_copy(it, 0, 1, TOP, 3, g_prev)

    def w_relay(it):
        arrived(W.at[it, 3, TOP, :], w_recv.at[it, 0])
        w_copy(it, 3, 2, TOP, 4, g_next)
        arrived(W.at[it, 1, LOW, :], w_recv.at[it, 1])
        w_copy(it, 1, 2, LOW, 5, g_prev)

    def w_near(it):
        arrived(W.at[it, 3, LOW, :], w_recv.at[it, 2])
        arrived(W.at[it, 1, TOP, :], w_recv.at[it, 3])

    def w_far(it):
        arrived(W.at[it, 2, TOP, :], w_recv.at[it, 4])
        arrived(W.at[it, 2, LOW, :], w_recv.at[it, 5])

    def residual(it, wave, slots, first):
        rows = pl.ds(wave * WAVE, WAVE)
        total = None
        for slot in slots:
            part = jnp.dot(X[slot, rows, :], W[it, slot], preferred_element_type=jnp.float32)
            total = part if total is None else total + part
        Racc[rows, :] = total if first else Racc[rows, :] + total

    def chunk(wave, d):
        return pl.multiple_of(wave * WAVE + lax.rem(r + d, 4) * PIECE, 16)

    A, B = pl.ds(0, SPLIT), pl.ds(SPLIT, PIECE - SPLIT)

    def r_copy(it, wave, d, half, dst, index, to):
        return send(RS.at[it, wave, d - 1, half, :], dst, r_send.at[it, wave, index], r_recv.at[it, wave, index], to)

    def r_start(it, wave):
        RS[it, wave, 1] = Racc[pl.ds(chunk(wave, 2), PIECE), :].astype(jnp.bfloat16)
        r_copy(it, wave, 2, A, RCA.at[it, wave], 0, r_next)
        r_copy(it, wave, 2, B, RCB.at[it, wave], 1, r_prev)
        RS[it, wave, 0, B, :] = Racc[pl.ds(pl.multiple_of(chunk(wave, 1) + SPLIT, 16), PIECE - SPLIT), :].astype(jnp.bfloat16)
        r_copy(it, wave, 1, B, RFP.at[it, wave, B, :], 2, r_next)
        RS[it, wave, 2, A, :] = Racc[pl.ds(chunk(wave, 3), SPLIT), :].astype(jnp.bfloat16)
        r_copy(it, wave, 3, A, RFM.at[it, wave, A, :], 3, r_prev)

    def r_middle(it, wave):
        arrived(RCA.at[it, wave], r_recv.at[it, wave, 0])
        RS[it, wave, 0, A, :] = (
            Racc[pl.ds(chunk(wave, 1), SPLIT), :] + RCA[it, wave].astype(jnp.float32)
        ).astype(jnp.bfloat16)
        r_copy(it, wave, 1, A, RFP.at[it, wave, A, :], 4, r_next)
        arrived(RCB.at[it, wave], r_recv.at[it, wave, 1])
        RS[it, wave, 2, B, :] = (
            Racc[pl.ds(pl.multiple_of(chunk(wave, 3) + SPLIT, 16), PIECE - SPLIT), :]
            + RCB[it, wave].astype(jnp.float32)
        ).astype(jnp.bfloat16)
        r_copy(it, wave, 3, B, RFM.at[it, wave, B, :], 5, r_prev)

    def e_copy(it, wave, d, half, index, to):
        start = chunk(wave, d) + (0 if half == 0 else SPLIT)
        rows = pl.ds(pl.multiple_of(start, 16), SPLIT if half == 0 else PIECE - SPLIT)
        return send(E.at[it, rows, :], E.at[it, rows, :], e_send.at[it, wave, index], e_recv.at[it, wave, index], to)

    def e_wait(it, wave, d, half, index):
        start = chunk(wave, d) + (0 if half == 0 else SPLIT)
        rows = pl.ds(pl.multiple_of(start, 16), SPLIT if half == 0 else PIECE - SPLIT)
        arrived(E.at[it, rows, :], e_recv.at[it, wave, index])

    def r_finish(it, wave):
        arrived(RFP.at[it, wave, B, :], r_recv.at[it, wave, 2])
        arrived(RFM.at[it, wave, A, :], r_recv.at[it, wave, 3])
        arrived(RFP.at[it, wave, A, :], r_recv.at[it, wave, 4])
        arrived(RFM.at[it, wave, B, :], r_recv.at[it, wave, 5])
        rows = pl.ds(chunk(wave, 0), PIECE)
        total = Racc[rows, :] + RFP[it, wave].astype(jnp.float32) + RFM[it, wave].astype(jnp.float32)
        E[it, rows, :] = (2.0 / TOKENS * total).astype(jnp.bfloat16)
        e_copy(it, wave, 0, 0, 0, r_next)
        e_copy(it, wave, 0, 1, 1, r_prev)
        e_copy(it, wave, 0, 1, 2, r_next)
        e_copy(it, wave, 0, 0, 3, r_prev)

    def e_relay(it, wave):
        e_wait(it, wave, 3, 0, 0)
        e_copy(it, wave, 3, 0, 4, r_next)
        e_wait(it, wave, 1, 1, 1)
        e_copy(it, wave, 1, 1, 5, r_prev)

    def e_end(it, wave):
        e_wait(it, wave, 3, 1, 2)
        e_wait(it, wave, 1, 0, 3)
        e_wait(it, wave, 2, 0, 4)
        e_wait(it, wave, 2, 1, 5)

    def gradient(it, wave, slot):
        rows = pl.ds(wave * WAVE, WAVE)
        part = lax.dot_general(
            X[slot, rows, :], E[it, rows, :], (((0,), (0,)), ((), ())), preferred_element_type=jnp.float32
        )
        Gacc[slot] = part if wave == 0 else Gacc[slot] + part

    def g_copy(it, d, half, dst, index, to):
        return send(GS.at[it, d - 1, half, :], dst, g_send.at[it, index], g_recv.at[it, index], to)

    def g_reduce(it):
        gradient(it, 1, 2)
        GS[it, 1] = Gacc[2].astype(jnp.bfloat16)
        g_copy(it, 2, TOP, GCA.at[it], 0, g_next)
        g_copy(it, 2, LOW, GCB.at[it], 1, g_prev)
        gradient(it, 1, 1)
        GS[it, 0, LOW, :] = Gacc[1, LOW, :].astype(jnp.bfloat16)
        g_copy(it, 1, LOW, GFP.at[it, LOW, :], 2, g_next)
        gradient(it, 1, 3)
        GS[it, 2, TOP, :] = Gacc[3, TOP, :].astype(jnp.bfloat16)
        g_copy(it, 3, TOP, GFM.at[it, TOP, :], 3, g_prev)
        arrived(GCA.at[it], g_recv.at[it, 0])
        GS[it, 0, TOP, :] = (Gacc[1, TOP, :] + GCA[it].astype(jnp.float32)).astype(jnp.bfloat16)
        g_copy(it, 1, TOP, GFP.at[it, TOP, :], 4, g_next)
        arrived(GCB.at[it], g_recv.at[it, 1])
        GS[it, 2, LOW, :] = (Gacc[3, LOW, :] + GCB[it].astype(jnp.float32)).astype(jnp.bfloat16)
        g_copy(it, 3, LOW, GFM.at[it, LOW, :], 5, g_prev)
        gradient(it, 1, 0)
        arrived(GFP.at[it, LOW, :], g_recv.at[it, 2])
        arrived(GFM.at[it, TOP, :], g_recv.at[it, 3])
        arrived(GFP.at[it, TOP, :], g_recv.at[it, 4])
        arrived(GFM.at[it, LOW, :], g_recv.at[it, 5])

    first_delta()
    w_start(0)
    for slot in range(RING):
        arrived(X.at[slot, pl.ds(0, PIECE), :], x1_recv.at[slot])
    for half in range(2):
        z_forward(1, 0, half)
        z_forward(-1, 0, 1 - half)
    w_relay(0)
    for half in range(2):
        z_wait(1, half)
        z_forward(1, 1, half)
        z_wait(2, 1 - half)
        z_forward(-1, 2, 1 - half)
    w_near(0)
    w_far(0)
    for half in range(2):
        z_wait(3, half)
        z_forward(1, 3, half)
        z_wait(4, 1 - half)
        z_forward(-1, 4, 1 - half)
    residual(0, 0, (0, 1, 2, 3), True)
    r_start(0, 0)
    r_middle(0, 0)
    r_finish(0, 0)
    z_wait(5, 0)
    z_forward(1, 5, 0)
    z_wait(6, 1)
    z_forward(-1, 6, 1)
    e_relay(0, 0)
    e_end(0, 0)
    for slot in range(RING):
        gradient(0, 0, slot)
    z_wait(5, 1)
    z_wait(6, 0)
    z_wait(7, 0)
    z_wait(7, 1)
    residual(0, 1, (0, 1, 2, 3), True)
    r_start(0, 1)
    r_middle(0, 1)
    r_finish(0, 1)
    e_relay(0, 1)
    e_end(0, 1)
    g_reduce(0)
    update(0)

    w_start(1)
    residual(1, 0, (0,), True)
    residual(1, 1, (0,), True)
    w_relay(1)
    w_near(1)
    residual(1, 0, (1, 3), False)
    residual(1, 1, (1, 3), False)
    w_far(1)
    residual(1, 0, (2,), False)
    r_start(1, 0)
    residual(1, 1, (2,), False)
    r_start(1, 1)
    r_middle(1, 0)
    r_middle(1, 1)
    r_finish(1, 0)
    r_finish(1, 1)
    e_relay(1, 0)
    e_relay(1, 1)
    e_end(1, 0)
    for slot in range(RING):
        gradient(1, 0, slot)
    e_end(1, 1)
    g_reduce(1)
    update(1)

    for copy in pending:
        copy.wait_send()
    for mine, remote in exchange:

        @pl.when(mine != 0)
        def _():
            remote.wait_send()


def per_device(tokens, weight, rounding, floor_codes, scale_codes, zero_codes, block_mask):
    scales = base_scale * jnp.exp2(scale_codes.astype(jnp.float32) * 0.25)
    zero_point = zero_codes.astype(jnp.float32)
    kept = jnp.repeat(block_mask.astype(jnp.float32), BLOCK, axis=1)
    whole = pl.BlockSpec(memory_space=pltpu.VMEM)
    bf16, f32 = jnp.bfloat16, jnp.float32
    dma = pltpu.SemaphoreType.DMA
    return pl.pallas_call(
        kernel,
        out_shape=jax.ShapeDtypeStruct((ROWS, COLS), f32),
        in_specs=[whole] * 7,
        out_specs=whole,
        scratch_shapes=[
            pltpu.VMEM((RING, 2 * WAVE, ROWS), bf16),
            pltpu.VMEM((ITERS, RING, ROWS, COLS), bf16),
            pltpu.VMEM((ITERS, 2, 3, PIECE, COLS), bf16),
            pltpu.VMEM((ITERS, 2, SPLIT, COLS), bf16),
            pltpu.VMEM((ITERS, 2, PIECE - SPLIT, COLS), bf16),
            pltpu.VMEM((ITERS, 2, PIECE, COLS), bf16),
            pltpu.VMEM((ITERS, 2, PIECE, COLS), bf16),
            pltpu.VMEM((ITERS, 2 * WAVE, COLS), bf16),
            pltpu.VMEM((2 * WAVE, COLS), f32),
            pltpu.VMEM((RING, ROWS, COLS), f32),
            pltpu.VMEM((ITERS, 3, ROWS, COLS), bf16),
            pltpu.VMEM((ITERS, HALF, COLS), bf16),
            pltpu.VMEM((ITERS, HALF, COLS), bf16),
            pltpu.VMEM((ITERS, ROWS, COLS), bf16),
            pltpu.VMEM((ITERS, ROWS, COLS), bf16),
            dma((4,)), dma((4,)), dma((16,)), dma((16,)),
            dma((ITERS, 6)), dma((ITERS, 6)),
            dma((ITERS, 2, 6)), dma((ITERS, 2, 6)),
            dma((ITERS, 2, 6)), dma((ITERS, 2, 6)),
            dma((ITERS, 6)), dma((ITERS, 6)),
        ],
        compiler_params=pltpu.CompilerParams(has_side_effects=True, vmem_limit_bytes=67043328),
    )(tokens, weight, rounding, floor_codes, scales[None, :], zero_point[None, :], kept)


def solution(mesh):
    placed = (
        P("dp", "loop"),
        P("loop", "dp"),
        P("loop", "dp"),
        P("loop", "dp"),
        P("dp"),
        P("dp"),
        P("loop", "dp"),
    )
    return jax.shard_map(
        per_device, mesh=mesh, in_specs=placed, out_specs=P("loop", "dp"), check_vma=False
    )
```

time: 365 us -> 193 us (0.53)
  waiting for transfers between devices: 299 us -> 0 us
  Pallas kernels: 0 us -> 186 us
  matrix products: 35.1 us -> 0 us
  between operations: 13.2 us -> 0.01 us
  local copies, waits for them, and re-layouts: 15.4 us -> 4.81 us
    psum x2 -> x0, waiting for transfers between devices: 265 us -> none  [per_device(): lax.psum(partial_sum.astype(jnp.bfloat16), 'loop').astype(jnp.float32)]
    pallas_call x0 -> x1, Pallas kernels: none -> 186 us  [per_device(): pl.pallas_call(kernel, out_shape=jax.ShapeDtypeStruct((ROWS, COLS), f32),...]
    dot_general x4 -> x0, matrix products: 35.1 us -> none  [the longest x2 18.9 us: token_product(): lax.dot_general(token_rows, scaled_err, (((0,), (0,)), ((), ())), preferr...]
    all_gather x1 -> x0, waiting for transfers between devices: 32.9 us -> none  [per_device(): gathered = lax.all_gather(tokens, 'dp', axis=0, tiled=True)]
    convert_element_type x2 -> x0, local copies, waits for them, and re-layouts: 4.46 us -> none  [expand(): spread.reshape(row_blocks * BLOCK, col_blocks * BLOCK).astype(jnp.float32)]
    unnamed x17 -> x1, local copies, waits for them, and re-layouts: 7.17 us -> 2.85 us
  transfers between devices with their start and end apart: 3 -> 0, of which waited for: 3 -> 0; matrix products, arithmetic and copies ran while one was open for 4% -> 0% of each run, Pallas kernels for 0% -> 0%
where the time goes in v1:
time: 193 us
  Pallas kernels  186 us (96%)
  local copies, waits for them, and re-layouts  4.81 us (2%)
  other arithmetic  2.07 us (1%)
    pallas_call x1, Pallas kernels, per_device(): pl.pallas_call(kernel, out_shape=jax.ShapeDtypeStruct((ROWS, COLS), f32),...  186 us

profile of v1, /device:TPU:2, one launch (start us, length us, event | category | flops | bytes accessed | tf_op | source)
XLA Modules:
  0.0 192.8 jit_solution(17467506435403189931)
XLA Ops:
  0.0 0.7 exponential_multiply_fusion
  0.7 0.6 broadcast_in_dim.9.sc
  1.3 0.7 convert_element_type.10
  2.0 0.6 broadcast_in_dim.10.zp
  2.6 0.7 convert_element_type.11
  3.3 0.1 broadcast_in_dim.11
  3.3 0.7 reshape.3.km
  4.0 185.9 %shard_map.73 = f32[512,896]{1,0:T(8,128)} custom-call(bf16[224,512]{1,0:T(8,128)(2,1)} %tok.1, bf16[512,896]{1,0:T(8,128)(2,1)} %wt.1, f32[512,896]{1,0:T(8,128)} %v_in.1, s32[512,896]{1,0:T(8,128)} %fl.1, f32[1,896]{1,0:T(1,128)} %broadcast_in_dim.9.sc, f32[1,896]{1,0:T(1,128)} %broadcast_in_dim.10.zp, f32[8,896]{1,0:T(8,128)} %reshape.3.km), custom_call_target="tpu_custom_call" | custom-call | tf_op jit(solution)/shard_map/pallas_call | solution.py:366
  189.9 2.8 %copy.9 = f32[512,896]{1,0:T(8,128)} copy(f32[512,896]{1,0:T(8,128)} %shard_map.73) | data formatting | bytes 3670016
